TPU v7x, 32 devices: a whole 2x2x4 slice. The times are simulated.
32 devices in a mesh: dom: 8 (over z, core), group: 4 (over y, x).
Axes of the slice: x: 2, y: 2, z: 4, core: 2. Of those that a mesh axis runs over, the one named last changes fastest.
Arguments:
- start: bfloat16 [64, 32768], P(None, ('dom', 'group')), may hold values from -8.1 to 8.1
- tiles: int32 [32, 32, 128, 128], P(('dom', 'group')), may hold values from 0 to 15
- row_ptr: int32 [32, 9], P(('dom', 'group')), may hold values from 0 to 32, as said below
- col_part: int32 [32, 32], P(('dom', 'group')), may hold values from 0 to 7
- col_local: int32 [32, 32], P(('dom', 'group')), may hold values from 0 to 31, as said below
- halo_list: int32 [8, 8, 4], P('dom'), may hold values from 0 to 31
Outputs:
- vectors: bfloat16 [64, 32768], P(None, ('dom', 'group'))
- ritz: float32 [64, 64], replicated
Inputs may be any that keep to these rules, and one draw needn't show every extreme that they name: `row_ptr`: each row is strictly increasing from 0, so every block row has one or more slots; its last entry is at most 32 and equals 32 on some device row. `col_local`: below 32 where col_part names the row's own partition, below 4 otherwise.
All inputs are finite; a program needn't handle non-finite values.
Results may differ from a plain program's by a relative error of at most 0.012.
Values may be sent and summed in bfloat16 or wider, within the bound.
A program may use at most 64 MiB of HBM per device.

v0:
```python
import jax
import jax.numpy as jnp
from jax import lax
from jax.sharding import PartitionSpec as P

ITERS = 2


def shards(start, tiles, row_ptr, col_part, col_local, halo_list):
    own = lax.axis_index("dom")
    n_dom = lax.axis_size("dom")
    n_group = lax.axis_size("group")
    width = start.shape[0]
    rows_dev = start.shape[1]
    block = tiles.shape[2]
    slots = tiles.shape[1]
    block_rows = rows_dev // block
    halo = halo_list.shape[2]
    in_part = block_rows * n_group
    total_rows = rows_dev * n_dom * n_group
    pointers = row_ptr[0]
    counts = (pointers[1:] - pointers[:-1]).astype(jnp.float32)
    row_scale = 1.0 / (4.0 * jnp.sqrt(block * counts))
    slot_ids = jnp.arange(slots, dtype=jnp.int32)
    member = (
        (slot_ids[None, :] >= pointers[:-1, None]) & (slot_ids[None, :] < pointers[1:, None])
    ).astype(jnp.float32)
    centred = (tiles[0].astype(jnp.float32) - 7.5).astype(jnp.bfloat16)
    parts = col_part[0]
    places = col_local[0]
    pool_index = jnp.where(parts == own, places, in_part + parts * halo + places)
    targets = halo_list[0]

    def apply_graph(current):
        shaped = current.reshape(width, block_rows, block)
        part_blocks = lax.all_gather(shaped, "group", axis=1, tiled=True)
        outgoing = jnp.take(part_blocks, targets.reshape(-1), axis=1).reshape(
            width, n_dom, halo, block
        )
        incoming = lax.all_to_all(outgoing, "dom", split_axis=1, concat_axis=1, tiled=True)
        pool = jnp.concatenate([part_blocks, incoming.reshape(width, n_dom * halo, block)], axis=1)
        picked = jnp.take(pool, pool_index, axis=1)
        products = jnp.einsum("ksj,sij->ksi", picked, centred, preferred_element_type=jnp.float32)
        summed = jnp.einsum("rs,ksi->kri", member, products, precision=lax.Precision.HIGHEST)
        return (summed * row_scale[None, :, None]).reshape(width, rows_dev)

    current = start
    for step in range(ITERS):
        image = apply_graph(current)
        rounded = image.astype(jnp.bfloat16)
        local_gram = jnp.einsum("kn,ln->kl", rounded, rounded, preferred_element_type=jnp.float32)
        gram = lax.psum(local_gram, ("dom", "group")) / total_rows
        lower = jnp.linalg.cholesky(gram)
        current = lax.linalg.triangular_solve(
            lower, rounded.astype(jnp.float32), left_side=True, lower=True
        ).astype(jnp.bfloat16)
    final = apply_graph(current)
    local_ritz = jnp.einsum(
        "kn,ln->kl", current.astype(jnp.float32), final, precision=lax.Precision.HIGHEST
    )
    ritz = lax.psum(local_ritz, ("dom", "group")) / total_rows
    return (current, ritz)


def solution(mesh):
    return jax.shard_map(
        shards,
        mesh=mesh,
        in_specs=(
            P(None, ("dom", "group")),
            P(("dom", "group"), None, None, None),
            P(("dom", "group"), None),
            P(("dom", "group"), None),
            P(("dom", "group"), None),
            P("dom", None, None),
        ),
        out_specs=(P(None, ("dom", "group")), P()),
        check_vma=False,
    )
```

profile of v0, /device:TPU:14, one launch (start us, length us, event | category | flops | bytes accessed | tf_op | source)
XLA Modules:
  0.0 251.3 jit_solution(2166994840800570479)
XLA Ops:
  0.7 0.8 copy.50
  1.5 0.1 reshape_squeeze.2
  1.7 9.1 %all_gather.9 = bf16[64,32,128]{2,0,1:T(8,128)(2,1)S(1)} all-gather(bf16[64,8,128]{2,0,1:T(8,128)(2,1)S(1)} %copy_bitcast_fusion.2), channel_id=1, replica_groups=mesh['dom'=8,'group'=4] {'group'}, dimensions={1}, use_global_device_ids=true | all-gather | bytes 655360 | tf_op jit(solution)/shard_map/all_gather | solution.py:36
  10.7 0.6 gather_fusion
  11.4 0.9 broadcast_select_fusion.2
  12.3 5.5 %all-to-all-start = ((bf16[64,8,4,128]{3,0,2,1:T(8,128)(2,1)}), bf16[64,8,4,128]{3,0,2,1:T(8,128)(2,1)S(1)}, u32[]{:S(2)}, u32[]{:S(2)}) async-start(bf16[64,8,4,128]{3,0,2,1:T(8,128)(2,1)} %bitcast.5), calls=%async_computation | async-start | bytes 1048576 | tf_op jit(solution)/shard_map/all_to_all | solution.py:40
  17.8 0.1 multiply_divide_fusion
  17.9 0.1 slice_bitcast_fusion.1
  17.9 11.9 %all-to-all-done = bf16[64,8,4,128]{3,0,2,1:T(8,128)(2,1)S(1)} async-done(((bf16[64,8,4,128]{3,0,2,1:T(8,128)(2,1)}), bf16[64,8,4,128]{3,0,2,1:T(8,128)(2,1)S(1)}, u32[]{:S(2)}, u32[]{:S(2)}) %all-to-all-start) | async-done | bytes 524320 | tf_op jit(solution)/shard_map/all_to_all | solution.py:40
  29.9 1.1 pad_maximum_fusion
  30.9 1.9 gather_fusion.1
  32.8 0.8 convolution_bitcast_fusion.2
  33.7 1.1 fusion.3
  34.7 0.2 convolution_bitcast_fusion.4
  34.9 42.8 %psum.21 = f32[64,64]{0,1:T(8,128)S(1)} all-reduce(f32[64,64]{0,1:T(8,128)S(1)} %convolution_bitcast_fusion.4), channel_id=1, replica_groups=mesh['dom'=8,'group'=4] {'dom','group'}, use_global_device_ids=true, to_apply=%region_0.3 | all-reduce | flops 4096 | bytes 32768 | tf_op jit(solution)/shard_map/psum | solution.py:52
  77.7 0.1 copy.55
  77.8 5.8 %cholesky.44 = f32[64,64]{1,0:T(8,128)S(1)} custom-call(f32[64,64]{1,0:T(8,128)S(1)} %fusion.35), custom_call_target="Cholesky" | custom-call | tf_op jit(solution)/shard_map/jit(cholesky)/cholesky | solution.py:53
  83.7 0.6 compare_reduce_fusion.1
  84.4 0.7 fusion.30
  85.0 4.9 %custom-call.6 = f32[1,64,64]{1,2,0:T(8,128)S(1)} custom-call(f32[1,64,64]{2,1,0:T(8,128)S(1)} %fusion.30), custom_call_target="InvertDiagBlocksLowerTriangular" | custom-call | tf_op jit(solution)/shard_map/triangular_solve/custom-call.0 | solution.py:54
  90.0 0.4 fusion.4
  90.4 9.7 %all_gather.10 = bf16[64,32,128]{2,0,1:T(8,128)(2,1)S(1)} all-gather(bf16[64,8,128]{2,0,1:T(8,128)(2,1)S(1)} %bitcast.125), channel_id=1, replica_groups=mesh['dom'=8,'group'=4] {'group'}, dimensions={1}, use_global_device_ids=true | all-gather | bytes 655360 | tf_op jit(solution)/shard_map/all_gather | solution.py:36
  100.1 0.6 gather_fusion.2
  100.8 0.1 broadcast_select_fusion.1
  100.9 16.2 %all_to_all.15 = bf16[64,8,4,128]{3,0,2,1:T(8,128)(2,1)S(1)} all-to-all(bf16[64,8,4,128]{3,0,2,1:T(8,128)(2,1)S(1)} %bitcast.118), channel_id=1, replica_groups=mesh['dom'=8,'group'=4] {'dom'}, dimensions={1} | all-to-all | bytes 1048576 | tf_op jit(solution)/shard_map/all_to_all | solution.py:40
  117.1 1.1 pad_maximum_fusion.1
  118.2 1.9 gather_fusion.3
  120.1 0.8 convolution_bitcast_fusion.1
  120.9 1.1 fusion.2
  122.0 0.2 convolution_bitcast_fusion.3
  122.2 41.9 %psum.22 = f32[64,64]{0,1:T(8,128)S(1)} all-reduce(f32[64,64]{0,1:T(8,128)S(1)} %convolution_bitcast_fusion.3), channel_id=1, replica_groups=mesh['dom'=8,'group'=4] {'dom','group'}, use_global_device_ids=true, to_apply=%region_3.0 | all-reduce | flops 4096 | bytes 32768 | tf_op jit(solution)/shard_map/psum | solution.py:52
  164.1 0.1 copy.61
  164.2 5.8 %cholesky.55 = f32[64,64]{1,0:T(8,128)S(1)} custom-call(f32[64,64]{1,0:T(8,128)S(1)} %fusion.33), custom_call_target="Cholesky" | custom-call | tf_op jit(solution)/shard_map/jit(cholesky)/cholesky | solution.py:53
  170.1 0.6 compare_reduce_fusion
  170.7 0.7 fusion.31
  171.4 4.9 %custom-call.7 = f32[1,64,64]{1,2,0:T(8,128)S(1)} custom-call(f32[1,64,64]{2,1,0:T(8,128)S(1)} %fusion.31), custom_call_target="InvertDiagBlocksLowerTriangular" | custom-call | tf_op jit(solution)/shard_map/triangular_solve/custom-call.0 | solution.py:54
  176.3 0.4 convolution_convert_fusion
  176.8 9.7 %all_gather.11 = bf16[64,32,128]{2,0,1:T(8,128)(2,1)S(1)} all-gather(bf16[64,8,128]{2,0,1:T(8,128)(2,1)S(1)} %copy_bitcast_fusion), channel_id=1, replica_groups=mesh['dom'=8,'group'=4] {'group'}, dimensions={1}, use_global_device_ids=true | all-gather | bytes 655360 | tf_op jit(solution)/shard_map/all_gather | solution.py:36
  186.5 0.6 gather_fusion.4
  187.2 0.1 broadcast_select_fusion
  187.3 16.2 %all_to_all.16 = bf16[64,8,4,128]{3,0,2,1:T(8,128)(2,1)S(1)} all-to-all(bf16[64,8,4,128]{3,0,2,1:T(8,128)(2,1)S(1)} %bitcast.117), channel_id=1, replica_groups=mesh['dom'=8,'group'=4] {'dom'}, dimensions={1} | all-to-all | bytes 1048576 | tf_op jit(solution)/shard_map/all_to_all | solution.py:40
  203.5 1.1 pad_maximum_fusion.2
  204.6 1.9 gather_fusion.5
  206.5 0.8 convolution_bitcast_fusion
  207.3 1.1 convolution_multiply_fusion
  208.4 0.3 fusion.18
  208.7 41.9 %psum.23 = f32[64,64]{0,1:T(8,128)S(1)} all-reduce(f32[64,64]{0,1:T(8,128)S(1)} %fusion.18), channel_id=1, replica_groups=mesh['dom'=8,'group'=4] {'dom','group'}, use_global_device_ids=true, to_apply=%region_4.0 | all-reduce | flops 4096 | bytes 32768 | tf_op jit(solution)/shard_map/psum | solution.py:61
  250.6 0.7 copy.65
  (29 shorter events, 0.3 us)
Async XLA Ops:
  0.6 1.0 copy-start
  0.6 17.1 %copy-start.5 = (s32[1,32]{1,0:T(1,128)S(1)}, s32[1,32]{1,0:T(1,128)}, u32[]{:S(2)}) copy-start(s32[1,32]{1,0:T(1,128)} %param.17) | copy-start | bytes 388
  0.7 17.1 %copy-start.4 = (s32[1,32]{1,0:T(1,128)S(1)}, s32[1,32]{1,0:T(1,128)}, u32[]{:S(2)}) copy-start(s32[1,32]{1,0:T(1,128)} %param.16) | copy-start | bytes 388
  0.7 17.1 %copy-start.3 = (s32[1,9]{1,0:T(1,128)S(1)}, s32[1,9]{1,0:T(1,128)}, u32[]{:S(2)}) copy-start(s32[1,9]{1,0:T(1,128)} %param.15) | copy-start | bytes 112
  12.3 20.5 %copy-start.1 = (s32[1,32,128,128]{3,2,1,0:T(8,128)S(1)}, s32[1,32,128,128]{3,2,1,0:T(8,128)}, u32[]{:S(2)}) copy-start(s32[1,32,128,128]{3,2,1,0:T(8,128)} %param.14) | copy-start | bytes 6291460
  12.3 17.6 %all-to-all-start = ((bf16[64,8,4,128]{3,0,2,1:T(8,128)(2,1)}), bf16[64,8,4,128]{3,0,2,1:T(8,128)(2,1)S(1)}, u32[]{:S(2)}, u32[]{:S(2)}) async-start(bf16[64,8,4,128]{3,0,2,1:T(8,128)(2,1)} %bitcast.5), calls=%async_computation | async-start | bytes 1048576 | tf_op jit(solution)/shard_map/all_to_all | solution.py:40
  176.7 31.7 %copy-start.2 = (bf16[64,1024]{1,0:T(8,128)(2,1)}, bf16[64,1024]{1,0:T(8,128)(2,1)S(1)}, u32[]{:S(2)}) copy-start(bf16[64,1024]{1,0:T(8,128)(2,1)S(1)} %convolution_convert_fusion) | copy-start | bytes 393220
where the time goes:
time: 252 us; the launch traced here: 251 us
  blocking collectives  187 us (74%)
  other arithmetic  28.7 us (11%)
  waiting for transfers between devices  11.9 us (5%)
  local copies, waits for them, and re-layouts  9.49 us (4%)
  matrix products  7.18 us (3%)
  starting transfers between devices  5.45 us (2%)
    psum x2, blocking collectives, shards(): gram = lax.psum(local_gram, ('dom', 'group')) / total_rows  84.7 us
    psum x1, blocking collectives, shards(): ritz = lax.psum(local_ritz, ('dom', 'group')) / total_rows  41.9 us
    all_to_all x2, blocking collectives, apply_graph(): lax.all_to_all(outgoing, 'dom', split_axis=1, concat_axis=1, tiled=True)  32.5 us
    all_gather x3, blocking collectives, apply_graph(): part_blocks = lax.all_gather(shaped, 'group', axis=1, tiled=True)  28.5 us
    another operation x6, other arithmetic, shards(): lower = jnp.linalg.cholesky(gram)  13 us
    all_to_all x1, waiting for transfers between devices, apply_graph(): lax.all_to_all(outgoing, 'dom', split_axis=1, concat_axis=1, tiled=True)  11.9 us
    another operation x4, other arithmetic, shards(): lax.linalg.triangular_solve(lower, rounded.astype(jnp.float32), left_side...  11.1 us
    gather x3, local copies, waits for them, and re-layouts, apply_graph(): picked = jnp.take(pool, pool_index, axis=1)  5.61 us
  transfers between devices with their start and end apart: 1, of which 1 were waited for; matrix products, arithmetic and copies ran while one was open for 0% of the time, Pallas kernels for 0%

commit v1 on v0

--- a/solution.py
+++ b/solution.py
@@ -7,6 +7,11 @@
 
 
 def shards(start, tiles, row_ptr, col_part, col_local, halo_list):
+
+    def search_the_group(obj):
+        h_now = jax.lax.all_gather(obj, ("dom", "group"))
+        return jnp.sum(h_now, 0)
+
     own = lax.axis_index("dom")
     n_dom = lax.axis_size("dom")
     n_group = lax.axis_size("group")
@@ -58,7 +63,7 @@
     local_ritz = jnp.einsum(
         "kn,ln->kl", current.astype(jnp.float32), final, precision=lax.Precision.HIGHEST
     )
-    ritz = lax.psum(local_ritz, ("dom", "group")) / total_rows
+    ritz = search_the_group(local_ritz) / total_rows
     return (current, ritz)
 
 

time: 252 us -> 285 us (1.13)
  the two profiles are of different devices: /device:TPU:14 before, /device:TPU:0 now
where the time goes in v1:
time: 285 us
  blocking collectives  218 us (76%)
  other arithmetic  28.8 us (10%)
  waiting for transfers between devices  15.1 us (5%)
  local copies, waits for them, and re-layouts  9.57 us (3%)
  matrix products  7.22 us (3%)
  starting transfers between devices  5.01 us (2%)
    psum x2, blocking collectives, shards(): gram = lax.psum(local_gram, ('dom', 'group')) / total_rows  74.5 us
    all_gather x1, blocking collectives, search_the_group(): h_now = jax.lax.all_gather(obj, ('dom', 'group'))  70.9 us
    all_to_all x2, blocking collectives, apply_graph(): lax.all_to_all(outgoing, 'dom', split_axis=1, concat_axis=1, tiled=True)  38.2 us
    all_gather x3, blocking collectives, apply_graph(): part_blocks = lax.all_gather(shaped, 'group', axis=1, tiled=True)  34.5 us
    all_to_all x1, waiting for transfers between devices, apply_graph(): lax.all_to_all(outgoing, 'dom', split_axis=1, concat_axis=1, tiled=True)  15.1 us
    another operation x6, other arithmetic, shards(): lower = jnp.linalg.cholesky(gram)  13 us
    another operation x4, other arithmetic, shards(): lax.linalg.triangular_solve(lower, rounded.astype(jnp.float32), left_side...  11.1 us
  transfers between devices with their start and end apart: 1, of which 1 were waited for; matrix products, arithmetic and copies ran while one was open for 0% of the time, Pallas kernels for 0%

profile of v1, /device:TPU:0, one launch (start us, length us, event | category | flops | bytes accessed | tf_op | source)
XLA Modules:
  0.0 284.8 jit_solution(6644377734615638734)
XLA Ops:
  0.7 0.8 copy.47
  1.5 0.1 reshape_squeeze.2
  1.7 11.5 %all_gather.15 = bf16[64,32,128]{2,0,1:T(8,128)(2,1)S(1)} all-gather(bf16[64,8,128]{2,0,1:T(8,128)(2,1)S(1)} %copy_bitcast_fusion.2), channel_id=1, replica_groups=mesh['dom'=8,'group'=4] {'group'}, dimensions={1}, use_global_device_ids=true | all-gather | bytes 655360 | tf_op jit(solution)/shard_map/all_gather | solution.py:41
  13.2 0.6 gather_fusion
  13.8 0.9 broadcast_select_fusion.2
  14.7 5.0 %all-to-all-start = ((bf16[64,8,4,128]{3,0,2,1:T(8,128)(2,1)}), bf16[64,8,4,128]{3,0,2,1:T(8,128)(2,1)S(1)}, u32[]{:S(2)}, u32[]{:S(2)}) async-start(bf16[64,8,4,128]{3,0,2,1:T(8,128)(2,1)} %bitcast.5), calls=%async_computation | async-start | bytes 1048576 | tf_op jit(solution)/shard_map/all_to_all | solution.py:45
  19.8 0.1 multiply_divide_fusion
  20.0 15.1 %all-to-all-done = bf16[64,8,4,128]{3,0,2,1:T(8,128)(2,1)S(1)} async-done(((bf16[64,8,4,128]{3,0,2,1:T(8,128)(2,1)}), bf16[64,8,4,128]{3,0,2,1:T(8,128)(2,1)S(1)}, u32[]{:S(2)}, u32[]{:S(2)}) %all-to-all-start) | async-done | bytes 524320 | tf_op jit(solution)/shard_map/all_to_all | solution.py:45
  35.1 1.1 pad_maximum_fusion
  36.2 1.9 gather_fusion.1
  38.1 0.8 convolution_bitcast_fusion.2
  38.9 1.1 fusion.3
  40.0 0.2 convolution_bitcast_fusion.4
  40.1 37.0 %psum.14 = f32[64,64]{0,1:T(8,128)S(1)} all-reduce(f32[64,64]{0,1:T(8,128)S(1)} %convolution_bitcast_fusion.4), channel_id=1, replica_groups=mesh['dom'=8,'group'=4] {'dom','group'}, use_global_device_ids=true, to_apply=%region_0.3 | all-reduce | flops 4096 | bytes 32768 | tf_op jit(solution)/shard_map/psum | solution.py:57
  77.3 5.8 %cholesky.44 = f32[64,64]{1,0:T(8,128)S(1)} custom-call(f32[64,64]{1,0:T(8,128)S(1)} %fusion.35), custom_call_target="Cholesky" | custom-call | tf_op jit(solution)/shard_map/jit(cholesky)/cholesky | solution.py:58
  83.1 0.6 compare_reduce_fusion.1
  83.8 0.7 fusion.30
  84.4 4.9 %custom-call.6 = f32[1,64,64]{1,2,0:T(8,128)S(1)} custom-call(f32[1,64,64]{2,1,0:T(8,128)S(1)} %fusion.30), custom_call_target="InvertDiagBlocksLowerTriangular" | custom-call | tf_op jit(solution)/shard_map/triangular_solve/custom-call.0 | solution.py:59
  89.4 0.4 fusion.4
  89.8 11.5 %all_gather.16 = bf16[64,32,128]{2,0,1:T(8,128)(2,1)S(1)} all-gather(bf16[64,8,128]{2,0,1:T(8,128)(2,1)S(1)} %bitcast.127), channel_id=1, replica_groups=mesh['dom'=8,'group'=4] {'group'}, dimensions={1}, use_global_device_ids=true | all-gather | bytes 655360 | tf_op jit(solution)/shard_map/all_gather | solution.py:41
  101.3 0.6 gather_fusion.2
  102.0 0.1 broadcast_select_fusion.1
  102.1 19.3 %all_to_all.15 = bf16[64,8,4,128]{3,0,2,1:T(8,128)(2,1)S(1)} all-to-all(bf16[64,8,4,128]{3,0,2,1:T(8,128)(2,1)S(1)} %bitcast.120), channel_id=1, replica_groups=mesh['dom'=8,'group'=4] {'dom'}, dimensions={1} | all-to-all | bytes 1048576 | tf_op jit(solution)/shard_map/all_to_all | solution.py:45
  121.4 1.1 pad_maximum_fusion.1
  122.5 1.9 gather_fusion.3
  124.4 0.8 convolution_bitcast_fusion.1
  125.2 1.1 fusion.2
  126.3 0.2 convolution_bitcast_fusion.3
  126.5 37.6 %psum.15 = f32[64,64]{0,1:T(8,128)S(1)} all-reduce(f32[64,64]{0,1:T(8,128)S(1)} %convolution_bitcast_fusion.3), channel_id=1, replica_groups=mesh['dom'=8,'group'=4] {'dom','group'}, use_global_device_ids=true, to_apply=%region_3.0 | all-reduce | flops 4096 | bytes 32768 | tf_op jit(solution)/shard_map/psum | solution.py:57
  164.1 0.1 copy.58
  164.2 5.8 %cholesky.55 = f32[64,64]{1,0:T(8,128)S(1)} custom-call(f32[64,64]{1,0:T(8,128)S(1)} %fusion.33), custom_call_target="Cholesky" | custom-call | tf_op jit(solution)/shard_map/jit(cholesky)/cholesky | solution.py:58
  170.0 0.6 compare_reduce_fusion
  170.7 0.7 fusion.31
  171.4 4.9 %custom-call.7 = f32[1,64,64]{1,2,0:T(8,128)S(1)} custom-call(f32[1,64,64]{2,1,0:T(8,128)S(1)} %fusion.31), custom_call_target="InvertDiagBlocksLowerTriangular" | custom-call | tf_op jit(solution)/shard_map/triangular_solve/custom-call.0 | solution.py:59
  176.3 0.4 convolution_convert_fusion
  176.8 11.5 %all_gather.17 = bf16[64,32,128]{2,0,1:T(8,128)(2,1)S(1)} all-gather(bf16[64,8,128]{2,0,1:T(8,128)(2,1)S(1)} %copy_bitcast_fusion), channel_id=1, replica_groups=mesh['dom'=8,'group'=4] {'group'}, dimensions={1}, use_global_device_ids=true | all-gather | bytes 655360 | tf_op jit(solution)/shard_map/all_gather | solution.py:41
  188.2 0.6 gather_fusion.4
  188.9 0.1 broadcast_select_fusion
  189.0 18.8 %all_to_all.16 = bf16[64,8,4,128]{3,0,2,1:T(8,128)(2,1)S(1)} all-to-all(bf16[64,8,4,128]{3,0,2,1:T(8,128)(2,1)S(1)} %bitcast.119), channel_id=1, replica_groups=mesh['dom'=8,'group'=4] {'dom'}, dimensions={1} | all-to-all | bytes 1048576 | tf_op jit(solution)/shard_map/all_to_all | solution.py:45
  207.8 1.1 pad_maximum_fusion.2
  208.9 1.9 gather_fusion.5
  210.8 0.8 convolution_bitcast_fusion
  211.6 1.1 convolution_multiply_fusion
  212.7 0.3 fusion.18
  213.0 70.9 %all-gather = f32[2048,64]{1,0:T(8,128)S(1)} all-gather(f32[64,64]{1,0:T(8,128)S(1)} %fusion.18), channel_id=2, replica_groups=mesh['dom'=8,'group'=4] {'dom','group'}, dimensions={0}, use_global_device_ids=true | all-gather | bytes 540672 | tf_op jit(solution)/shard_map/all_gather | solution.py:12
  283.9 0.1 reduce_sum.9
  284.0 0.1 copy.61
  284.1 0.7 copy.62
  (31 shorter events, 0.5 us)
Async XLA Ops:
  0.6 1.0 copy-start
  0.6 19.1 %copy-start.5 = (s32[1,32]{1,0:T(1,128)S(1)}, s32[1,32]{1,0:T(1,128)}, u32[]{:S(2)}) copy-start(s32[1,32]{1,0:T(1,128)} %param.17) | copy-start | bytes 388
  0.7 19.1 %copy-start.4 = (s32[1,32]{1,0:T(1,128)S(1)}, s32[1,32]{1,0:T(1,128)}, u32[]{:S(2)}) copy-start(s32[1,32]{1,0:T(1,128)} %param.16) | copy-start | bytes 388
  0.7 19.1 %copy-start.3 = (s32[1,9]{1,0:T(1,128)S(1)}, s32[1,9]{1,0:T(1,128)}, u32[]{:S(2)}) copy-start(s32[1,9]{1,0:T(1,128)} %param.15) | copy-start | bytes 112
  14.7 23.3 %copy-start.1 = (s32[1,32,128,128]{3,2,1,0:T(8,128)S(1)}, s32[1,32,128,128]{3,2,1,0:T(8,128)}, u32[]{:S(2)}) copy-start(s32[1,32,128,128]{3,2,1,0:T(8,128)} %param.14) | copy-start | bytes 6291460
  14.7 20.3 %all-to-all-start = ((bf16[64,8,4,128]{3,0,2,1:T(8,128)(2,1)}), bf16[64,8,4,128]{3,0,2,1:T(8,128)(2,1)S(1)}, u32[]{:S(2)}, u32[]{:S(2)}) async-start(bf16[64,8,4,128]{3,0,2,1:T(8,128)(2,1)} %bitcast.5), calls=%async_computation | async-start | bytes 1048576 | tf_op jit(solution)/shard_map/all_to_all | solution.py:45
  176.7 36.0 %copy-start.2 = (bf16[64,1024]{1,0:T(8,128)(2,1)}, bf16[64,1024]{1,0:T(8,128)(2,1)S(1)}, u32[]{:S(2)}) copy-start(bf16[64,1024]{1,0:T(8,128)(2,1)S(1)} %convolution_convert_fusion) | copy-start | bytes 393220
